TPU v7x, 256 devices: a whole 4x4x8 slice. The times are simulated.
256 devices in a mesh: dp: 16 (over y, z_hi, core), mp: 16 (over x, z_lo).
Axes of the slice: x: 4, y: 4, z: 8 (z_hi: 2, z_lo: 4; z = z_hi * 4 + z_lo), core: 2. Of those that a mesh axis runs over, the one named last changes fastest.
Arguments:
- skip_stream_arriving: float32 [4096, 2304], P('dp', 'mp'), may hold values from -170 to 170
- chosen_specialists: int32 [4096, 2], P('dp'), may hold values from 0 to 3, all different within a row; in each aligned block of 256 rows (0 to 255, 256 to 511, ...) at most 160 rows name the same one
- sequence_piece_tallies: int32 [16, 4], P('dp'), may hold values from 1 to 128, 256 in all within a row
- premix_rmsnorm_gain: float32 [2304], P('mp'), may hold values from 0.1 to 1.9
- dispatcher_weights: bfloat16 [2304, 4], replicated, may hold values from -0.125 to 0.125
- specialist_switch_weights: bfloat16 [4, 2304, 5760], P(None, 'dp', 'mp'), may hold values from -0.125 to 0.125
- specialist_expand_weights: bfloat16 [4, 2304, 5760], P(None, 'dp', 'mp'), may hold values from -0.125 to 0.125
- specialist_contract_weights: bfloat16 [4, 5760, 2304], P(None, 'mp', 'dp'), may hold values from -0.109375 to 0.109375
- terminal_rmsnorm_gain: float32 [2304], replicated, may hold values from 0.1 to 1.9
- lexicon_projector_weights: bfloat16 [2304, 131072], P(None, ('dp', 'mp')), may hold values from -12 to 12
- softness_per_sequence: float32 [64], replicated, may hold values from 0.02 to 1.5
Outputs:
- new_hidden: float32 [4096, 2304], P('dp', 'mp')
- logprobs: float32 [64, 131072], P(None, ('dp', 'mp'))
Inputs may be any that keep to these rules, and one draw needn't show every extreme that they name: `chosen_specialists`: in the 256 rows of each data group no expert is named by more than 160 rows, a bound that some block reaches. `sequence_piece_tallies`: each row sums to 256; its largest entry is 128.
All inputs are finite; a program needn't handle non-finite values.
Results may differ from a plain program's by a relative error of at most 0.0014.
Values may be sent and summed in bfloat16 or wider, within the bound.
A program may use at most 128 MiB of HBM per device.

v0:
```python
import math
import jax
import jax.numpy as jnp
from jax import lax
from jax.sharding import PartitionSpec as P

EMBED_DIMENSION = 2304
CAP = 160
branch_scale = 1.4 / math.sqrt(40.0)
epsilon = 1e-05


def slot_tables(routes_grp, expert, capacity):
    count = routes_grp.shape[0]
    hit = jnp.any(routes_grp == expert, axis=1)
    second = (routes_grp[:, 1] == expert).astype(jnp.int32)
    order = jnp.cumsum(hit.astype(jnp.int32), dtype=jnp.int32) - 1
    target = jnp.where(hit, order, capacity)
    tokens = jnp.arange(count, dtype=jnp.int32)
    slot_rows = jnp.zeros((capacity,), jnp.int32).at[target].set(tokens, mode="drop")
    live = jnp.zeros((capacity,), jnp.float32).at[target].set(1.0, mode="drop")
    which = jnp.zeros((capacity,), jnp.int32).at[target].set(second, mode="drop")
    return (slot_rows, live, which)


def body(
    skip_stream_arriving,
    chosen_specialists,
    sequence_piece_tallies,
    premix_rmsnorm_gain,
    dispatcher_weights,
    specialist_switch_weights,
    specialist_expand_weights,
    specialist_contract_weights,
    terminal_rmsnorm_gain,
    lexicon_projector_weights,
    softness_per_sequence,
):
    tok_rows = skip_stream_arriving.shape[0]
    local_width = skip_stream_arriving.shape[1]
    experts = specialist_switch_weights.shape[0]
    unit_cols = specialist_switch_weights.shape[2]
    squares = lax.psum(jnp.sum(skip_stream_arriving * skip_stream_arriving, axis=1), "mp")
    normed_local = (
        skip_stream_arriving
        * lax.rsqrt(squares / EMBED_DIMENSION + epsilon)[:, None]
        * premix_rmsnorm_gain
    ).astype(jnp.bfloat16)
    features = lax.all_gather(normed_local, "mp", axis=1, tiled=True)
    router = jnp.dot(features, dispatcher_weights, preferred_element_type=jnp.float32)
    mixing = jax.nn.softmax(jnp.take_along_axis(router, chosen_specialists, axis=1), axis=1)
    tables = [slot_tables(chosen_specialists, expert, CAP) for expert in range(experts)]
    inputs = jnp.stack([features[table[0]] for table in tables])
    scales = jnp.stack([mixing[table[0], table[2]] * table[1] for table in tables])
    pieces_out = []
    for expert in range(experts):
        rows_in = inputs[expert]

        def add_pair(carry, pieces, start, rows_in=rows_in):
            return (
                jnp.dot(rows_in, pieces[0], preferred_element_type=jnp.float32),
                jnp.dot(rows_in, pieces[1], preferred_element_type=jnp.float32),
            )

        empty = jnp.zeros((CAP, unit_cols), jnp.float32)
        gate, up_part = add_pair(
            (empty, empty),
            (
                lax.all_gather(specialist_switch_weights[expert], "dp", axis=0, tiled=True),
                lax.all_gather(specialist_expand_weights[expert], "dp", axis=0, tiled=True),
            ),
            jnp.int32(0),
        )
        act = (jax.nn.silu(gate) * up_part).astype(jnp.bfloat16)

        def project(piece, start, act=act):
            return jnp.dot(act, piece, preferred_element_type=jnp.float32)

        pieces_out.append(
            project(
                lax.all_gather(specialist_contract_weights[expert], "dp", axis=1, tiled=True),
                jnp.int32(0),
            )
        )
    outputs = jnp.stack(pieces_out)
    combined = jnp.zeros((tok_rows, EMBED_DIMENSION), jnp.float32)
    for expert in range(experts):
        combined = combined.at[tables[expert][0]].add(outputs[expert] * scales[expert][:, None])
    branch = lax.psum_scatter(
        combined.astype(jnp.bfloat16), "mp", scatter_dimension=1, tiled=True
    ).astype(jnp.float32)
    new_hidden = skip_stream_arriving + branch_scale * branch
    ends_index = jnp.cumsum(sequence_piece_tallies[0], dtype=jnp.int32) - 1
    end_local = new_hidden[ends_index]
    end_rows = lax.all_gather(end_local, "mp", axis=1, tiled=True)
    end_squares = jnp.sum(end_rows * end_rows, axis=1)
    end_normed = (
        end_rows
        * lax.rsqrt(end_squares / EMBED_DIMENSION + epsilon)[:, None]
        * terminal_rmsnorm_gain
    ).astype(jnp.bfloat16)
    lexicon_projector_feed = lax.all_gather(end_normed, "dp", axis=0, tiled=True)
    lexicon_logit_values = jnp.dot(
        lexicon_projector_feed, lexicon_projector_weights, preferred_element_type=jnp.float32
    ) / (EMBED_DIMENSION / 256.0 * softness_per_sequence[:, None])
    local_max = jnp.max(lexicon_logit_values, axis=1)
    local_sum = jnp.sum(jnp.exp(lexicon_logit_values - local_max[:, None]), axis=1)
    stats = jnp.stack([local_max, local_sum])
    for axis in ("mp", "dp"):
        held = lax.all_gather(stats, axis, axis=0)
        top = jnp.max(held[:, 0], axis=0)
        stats = jnp.stack([top, jnp.sum(held[:, 1] * jnp.exp(held[:, 0] - top[None]), axis=0)])
    largest, total_exp = (stats[0], stats[1])
    logprobs = lexicon_logit_values - largest[:, None] - jnp.log(total_exp)[:, None]
    return (new_hidden, logprobs)


def solution(mesh):
    return jax.shard_map(
        body,
        mesh=mesh,
        in_specs=(
            P("dp", "mp"),
            P("dp", None),
            P("dp", None),
            P("mp"),
            P(),
            P(None, "dp", "mp"),
            P(None, "dp", "mp"),
            P(None, "mp", "dp"),
            P(),
            P(None, ("dp", "mp")),
            P(),
        ),
        out_specs=(P("dp", "mp"), P(None, ("dp", "mp"))),
        check_vma=False,
    )
```

profile of v0, /device:TPU:1, one launch (start us, length us, event | category | flops | bytes accessed | tf_op | source)
XLA Modules:
  0.0 1087.2 jit_solution(11176963548852286973)
XLA Ops:
  8.4 38.4 %psum.7 = f32[256]{0:T(256)S(1)} all-reduce(f32[256]{0:T(256)S(1)} %multiply_reduce_fusion), channel_id=1, replica_groups=mesh['dp'=16,'mp'=16] {'mp'}, use_global_device_ids=true, to_apply=%region_5.6 | all-reduce | flops 256 | bytes 2048 | tf_op jit(solution)/shard_map/psum | solution.py:43
  83.7 43.5 %all-gather.33.cloned.1.call-done = bf16[256,2304]{0,1:T(8,128)(2,1)} async-done(((bf16[256,144]{0,1:T(8,128)(2,1)}), bf16[256,2304]{0,1:T(8,128)(2,1)}) %all-gather.33.cloned.1.call-update) | async-done | bytes 1179664 | tf_op jit(solution)/shard_map/all_gather | solution.py:49
  128.7 4.9 gather_fusion.9
  157.0 41.8 %all-gather.35.cloned.1.call-done = bf16[1,2304,360]{2,1,0:T(8,128)(2,1)} async-done(((bf16[1,144,360]{2,1,0:T(8,128)(2,1)}), bf16[1,2304,360]{2,1,0:T(8,128)(2,1)}) %all-gather.35.cloned.1.call-update) | async-done | bytes 1658896 | tf_op jit(solution)/shard_map/all_gather | solution.py:69
  201.0 56.7 %all-gather.37.cloned.1.call-done = bf16[1,2304,360]{2,1,0:T(8,128)(2,1)} async-done(((bf16[1,144,360]{2,1,0:T(8,128)(2,1)}), bf16[1,2304,360]{2,1,0:T(8,128)(2,1)}) %all-gather.37.cloned.1.call-update) | async-done | bytes 1658896 | tf_op jit(solution)/shard_map/all_gather | solution.py:70
  257.8 58.8 %all-gather.39.cloned.1.call-done = bf16[1,360,2304]{1,2,0:T(8,128)(2,1)} async-done(((bf16[1,360,144]{1,2,0:T(8,128)(2,1)}), bf16[1,360,2304]{1,2,0:T(8,128)(2,1)}) %all-gather.39.cloned.1.call-update) | async-done | bytes 1658896 | tf_op jit(solution)/shard_map/all_gather | solution.py:81
  321.0 5.0 scatter_custom_fusion.3
  326.1 49.4 %all-gather.41.cloned.1.call-done = bf16[1,2304,360]{2,1,0:T(8,128)(2,1)} async-done(((bf16[1,144,360]{2,1,0:T(8,128)(2,1)}), bf16[1,2304,360]{2,1,0:T(8,128)(2,1)}) %all-gather.41.cloned.1.call-update) | async-done | bytes 1658896 | tf_op jit(solution)/shard_map/all_gather | solution.py:69
  377.4 56.8 %all-gather.43.cloned.1.call-done = bf16[1,2304,360]{2,1,0:T(8,128)(2,1)} async-done(((bf16[1,144,360]{2,1,0:T(8,128)(2,1)}), bf16[1,2304,360]{2,1,0:T(8,128)(2,1)}) %all-gather.43.cloned.1.call-update) | async-done | bytes 1658896 | tf_op jit(solution)/shard_map/all_gather | solution.py:70
  434.2 59.5 %all-gather.45.cloned.1.call-done = bf16[1,360,2304]{1,2,0:T(8,128)(2,1)} async-done(((bf16[1,360,144]{1,2,0:T(8,128)(2,1)}), bf16[1,360,2304]{1,2,0:T(8,128)(2,1)}) %all-gather.45.cloned.1.call-update) | async-done | bytes 1658896 | tf_op jit(solution)/shard_map/all_gather | solution.py:81
  498.2 6.6 scatter_fusion
  504.7 48.0 %all-gather.47.cloned.1.call-done = bf16[1,2304,360]{2,1,0:T(8,128)(2,1)} async-done(((bf16[1,144,360]{2,1,0:T(8,128)(2,1)}), bf16[1,2304,360]{2,1,0:T(8,128)(2,1)}) %all-gather.47.cloned.1.call-update) | async-done | bytes 1658896 | tf_op jit(solution)/shard_map/all_gather | solution.py:69
  554.8 56.9 %all-gather.49.cloned.1.call-done = bf16[1,2304,360]{2,1,0:T(8,128)(2,1)} async-done(((bf16[1,144,360]{2,1,0:T(8,128)(2,1)}), bf16[1,2304,360]{2,1,0:T(8,128)(2,1)}) %all-gather.49.cloned.1.call-update) | async-done | bytes 1658896 | tf_op jit(solution)/shard_map/all_gather | solution.py:70
  611.8 58.8 %all-gather.51.cloned.1.call-done = bf16[1,360,2304]{1,2,0:T(8,128)(2,1)} async-done(((bf16[1,360,144]{1,2,0:T(8,128)(2,1)}), bf16[1,360,2304]{1,2,0:T(8,128)(2,1)}) %all-gather.51.cloned.1.call-update) | async-done | bytes 1658896 | tf_op jit(solution)/shard_map/all_gather | solution.py:81
  675.0 6.6 scatter_fusion.1
  681.5 48.0 %all-gather.53.cloned.1.call-done = bf16[1,2304,360]{2,1,0:T(8,128)(2,1)} async-done(((bf16[1,144,360]{2,1,0:T(8,128)(2,1)}), bf16[1,2304,360]{2,1,0:T(8,128)(2,1)}) %all-gather.53.cloned.1.call-update) | async-done | bytes 1658896 | tf_op jit(solution)/shard_map/all_gather | solution.py:69
  731.6 56.8 %all-gather.55.cloned.1.call-done = bf16[1,2304,360]{2,1,0:T(8,128)(2,1)} async-done(((bf16[1,144,360]{2,1,0:T(8,128)(2,1)}), bf16[1,2304,360]{2,1,0:T(8,128)(2,1)}) %all-gather.55.cloned.1.call-update) | async-done | bytes 1658896 | tf_op jit(solution)/shard_map/all_gather | solution.py:70
  788.4 59.5 %all-gather.57.cloned.1.call-done = bf16[1,360,2304]{1,2,0:T(8,128)(2,1)} async-done(((bf16[1,360,144]{1,2,0:T(8,128)(2,1)}), bf16[1,360,2304]{1,2,0:T(8,128)(2,1)}) %all-gather.57.cloned.1.call-update) | async-done | bytes 1658896 | tf_op jit(solution)/shard_map/all_gather | solution.py:81
  852.3 6.5 scatter_fusion.2
  863.3 70.4 %reduce-scatter.4.cloned.1.call-done = bf16[144,256]{1,0:T(8,128)(2,1)} async-done(((bf16[2304,256]{1,0:T(8,128)(2,1)}), bf16[144,256]{1,0:T(8,128)(2,1)}) %reduce-scatter.4.cloned.1.call-update) | async-done | bytes 73744
  936.1 31.2 %all-gather.15 = f32[16,144,4]{1,2,0:T(4,128)S(1)} all-gather(f32[1,144,4]{1,2,0:T(4,128)S(1)} %bitcast.132), channel_id=14, replica_groups=mesh['dp'=16,'mp'=16] {'mp'}, dimensions={0}, use_global_device_ids=true | all-gather | bytes 39168 | tf_op jit(solution)/shard_map/all_gather | solution.py:95
  967.7 50.6 %all-gather.16 = bf16[16,4,2304]{2,1,0:T(4,128)(2,1)S(1)} all-gather(bf16[1,4,2304]{2,1,0:T(4,128)(2,1)S(1)} %fusion.78), channel_id=1, replica_groups=mesh['dp'=16,'mp'=16] {'dp'}, dimensions={0}, use_global_device_ids=true | all-gather | bytes 313344 | tf_op jit(solution)/shard_map/all_gather | solution.py:102
  1019.2 29.8 %all-gather.17 = f32[16,2,64]{2,1,0:T(2,128)S(1)} all-gather(f32[1,2,64]{2,1,0:T(2,128)S(1)} %maximum_bitcast_fusion), channel_id=15, replica_groups=mesh['dp'=16,'mp'=16] {'mp'}, dimensions={0}, use_global_device_ids=true | all-gather | bytes 8704 | tf_op jit(solution)/shard_map/all_gather | solution.py:110
  1049.1 30.7 %all-gather.18 = f32[16,2,64]{2,1,0:T(2,128)S(1)} all-gather(f32[1,2,64]{2,1,0:T(2,128)S(1)} %maximum_bitcast_fusion.1), channel_id=16, replica_groups=mesh['dp'=16,'mp'=16] {'dp'}, dimensions={0}, use_global_device_ids=true | all-gather | bytes 8704 | tf_op jit(solution)/shard_map/all_gather | solution.py:110
  (180 shorter events, 97.4 us)
Async XLA Ops:
  7.2 1011.2 %copy-start = (bf16[2304,512]{1,0:T(8,128)(2,1)S(1)}, bf16[2304,512]{1,0:T(8,128)(2,1)}, u32[]{:S(2)}) copy-start(bf16[2304,512]{1,0:T(8,128)(2,1)} %param.20) | copy-start | bytes 7077892
  7.2 45.2 %copy-start.5 = (bf16[4,360,144]{1,2,0:T(8,128)(2,1)S(1)}, bf16[4,360,144]{1,2,0:T(8,128)(2,1)}, u32[]{:S(2)}) copy-start(bf16[4,360,144]{1,2,0:T(8,128)(2,1)} %param.18) | copy-start | bytes 1244164
  7.2 120.0 %all-gather.33.cloned.1.call-start = ((), (), s32[]{:S(2)}) async-start(), calls=%async_computation.1 | async-start | bytes 1253376 | tf_op jit(solution)/shard_map/all_gather | solution.py:49
  48.5 150.3 %all-gather.35.cloned.1.call-start = ((), (), s32[]{:S(2)}) async-start(), calls=%async_computation.2 | async-start | bytes 1880064 | tf_op jit(solution)/shard_map/all_gather | solution.py:69
  50.4 76.8 %copy-start.7 = (bf16[2304,4]{0,1:T(4,128)(2,1)S(1)}, bf16[2304,4]{0,1:T(4,128)(2,1)}, u32[]{:S(2)}) copy-start(bf16[2304,4]{0,1:T(4,128)(2,1)} %param.15) | copy-start | bytes 55300
  50.4 207.4 %all-gather.37.cloned.1.call-start = ((), (), s32[]{:S(2)}) async-start(), calls=%async_computation.3 | async-start | bytes 1880064 | tf_op jit(solution)/shard_map/all_gather | solution.py:70
  52.3 264.3 %all-gather.39.cloned.1.call-start = ((), (), s32[]{:S(2)}) async-start(), calls=%async_computation.4 | async-start | bytes 1880064 | tf_op jit(solution)/shard_map/all_gather | solution.py:81
  53.2 322.2 %all-gather.41.cloned.1.call-start = ((), (), s32[]{:S(2)}) async-start(), calls=%async_computation.5 | async-start | bytes 1880064 | tf_op jit(solution)/shard_map/all_gather | solution.py:69
  53.8 380.5 %all-gather.43.cloned.1.call-start = ((), (), s32[]{:S(2)}) async-start(), calls=%async_computation.6 | async-start | bytes 1880064 | tf_op jit(solution)/shard_map/all_gather | solution.py:70
  54.3 439.5 %all-gather.45.cloned.1.call-start = ((), (), s32[]{:S(2)}) async-start(), calls=%async_computation.7 | async-start | bytes 1880064 | tf_op jit(solution)/shard_map/all_gather | solution.py:81
  55.1 497.7 %all-gather.47.cloned.1.call-start = ((), (), s32[]{:S(2)}) async-start(), calls=%async_computation.8 | async-start | bytes 1880064 | tf_op jit(solution)/shard_map/all_gather | solution.py:69
  55.8 555.9 %all-gather.49.cloned.1.call-start = ((), (), s32[]{:S(2)}) async-start(), calls=%async_computation.9 | async-start | bytes 1880064 | tf_op jit(solution)/shard_map/all_gather | solution.py:70
  56.6 614.0 %all-gather.51.cloned.1.call-start = ((), (), s32[]{:S(2)}) async-start(), calls=%async_computation.10 | async-start | bytes 1880064 | tf_op jit(solution)/shard_map/all_gather | solution.py:81
  57.2 672.4 %all-gather.53.cloned.1.call-start = ((), (), s32[]{:S(2)}) async-start(), calls=%async_computation.11 | async-start | bytes 1880064 | tf_op jit(solution)/shard_map/all_gather | solution.py:69
  57.9 730.5 %all-gather.55.cloned.1.call-start = ((), (), s32[]{:S(2)}) async-start(), calls=%async_computation.12 | async-start | bytes 1880064 | tf_op jit(solution)/shard_map/all_gather | solution.py:70
  58.5 789.5 %all-gather.57.cloned.1.call-start = ((), (), s32[]{:S(2)}) async-start(), calls=%async_computation.13 | async-start | bytes 1880064 | tf_op jit(solution)/shard_map/all_gather | solution.py:81
  59.2 874.5 %reduce-scatter.4.cloned.1.call-start = ((), (), s32[]{:S(2)}) async-start(), calls=%async_computation.14 | async-start | bytes 1253376
  154.2 162.4 %copy-start.4 = (bf16[160,2304]{1,0:T(8,128)(2,1)S(1)}, bf16[160,2304]{1,0:T(8,128)(2,1)}, u32[]{:S(2)}) copy-start(bf16[160,2304]{1,0:T(8,128)(2,1)} %gather_fusion) | copy-start | bytes 2211844
  321.0 54.4 %copy-start.3 = (bf16[160,2304]{1,0:T(8,128)(2,1)S(1)}, bf16[160,2304]{1,0:T(8,128)(2,1)}, u32[]{:S(2)}) copy-start(bf16[160,2304]{1,0:T(8,128)(2,1)} %gather_fusion.2) | copy-start | bytes 2211844
  498.2 54.6 %copy-start.2 = (bf16[160,2304]{1,0:T(8,128)(2,1)S(1)}, bf16[160,2304]{1,0:T(8,128)(2,1)}, u32[]{:S(2)}) copy-start(bf16[160,2304]{1,0:T(8,128)(2,1)} %gather_fusion.4) | copy-start | bytes 2211844
  554.8 120.2 %copy-start.12 = (s32[160]{0:T(256)S(1)}, s32[160]{0:T(256)}, u32[]{:S(2)}) copy-start(s32[160]{0:T(256)} %copy-done.11) | copy-start | bytes 1924
  675.0 54.6 %copy-start.1 = (bf16[160,2304]{1,0:T(8,128)(2,1)S(1)}, bf16[160,2304]{1,0:T(8,128)(2,1)}, u32[]{:S(2)}) copy-start(bf16[160,2304]{1,0:T(8,128)(2,1)} %gather_fusion.6) | copy-start | bytes 2211844
  731.6 120.7 %copy-start.10 = (s32[160]{0:T(256)S(1)}, s32[160]{0:T(256)}, u32[]{:S(2)}) copy-start(s32[160]{0:T(256)} %copy-done.9) | copy-start | bytes 1924
  862.0 105.6 %copy-start.8 = (f32[2304]{0:T(1024)S(1)}, f32[2304]{0:T(1024)}, u32[]{:S(2)}) copy-start(f32[2304]{0:T(1024)} %param.19) | copy-start | bytes 27652
  (8 other events, 68.0 us)
Sparse Core Ops, SparseCore 0:
  48.6 78.5 all-gather.32
  129.8 68.9 all-gather.34
  201.4 56.3 all-gather.36
  260.2 56.3 all-gather.38
  319.0 56.3 all-gather.40
  377.9 56.3 all-gather.42
  437.4 56.3 all-gather.44
  496.4 56.3 all-gather.46
  555.4 56.3 all-gather.48
  614.2 56.3 all-gather.50
  673.2 56.3 all-gather.52
  732.0 56.3 all-gather.54
  791.6 56.3 all-gather.56
  862.2 71.5 reduce-scatter.3
where the time goes:
time: 1090 us
  waiting for transfers between devices  771 us (71%)
  blocking collectives  181 us (17%)
  local copies, waits for them, and re-layouts  55 us (5%)
  other arithmetic  37.7 us (3%)
  matrix products  28 us (3%)
  between operations  14.4 us (1%)
    all_gather x4, waiting for transfers between devices, body(): lax.all_gather(specialist_contract_weights[expert], 'dp', axis=1, tiled=T...  237 us
    all_gather x4, waiting for transfers between devices, body(): lax.all_gather(specialist_expand_weights[expert], 'dp', axis=0, tiled=True)  227 us
    all_gather x4, waiting for transfers between devices, body(): lax.all_gather(specialist_switch_weights[expert], 'dp', axis=0, tiled=True)  187 us
    unnamed x15, waiting for transfers between devices  76.1 us
    all_gather x2, blocking collectives, body(): held = lax.all_gather(stats, axis, axis=0)  60.5 us
    all_gather x1, blocking collectives, body(): lax.all_gather(end_normed, 'dp', axis=0, tiled=True)  50.6 us
    all_gather x1, waiting for transfers between devices, body(): features = lax.all_gather(normed_local, 'mp', axis=1, tiled=True)  43.5 us
    psum x1, blocking collectives, body(): lax.psum(jnp.sum(skip_stream_arriving * skip_stream_arriving, axis=1), 'mp')  38.4 us
  transfers between devices with their start and end apart: 14, of which 14 were waited for; matrix products, arithmetic and copies ran while one was open for 9% of the time, Pallas kernels for 0%

commit v1 on v0

--- a/solution.py
+++ b/solution.py
@@ -8,6 +8,13 @@
 CAP = 160
 branch_scale = 1.4 / math.sqrt(40.0)
 epsilon = 1e-05
+
+
+def _feed_squares(work_x):
+    w_next = lax.all_to_all(
+        jnp.stack([work_x for _ in range(lax.psum(1, axis_name="dp"))], 0), "dp", 0, 0
+    )
+    return jnp.concatenate(w_next, 1)
 
 
 def slot_tables(routes_grp, expert, capacity):
@@ -76,12 +83,7 @@
         def project(piece, start, act=act):
             return jnp.dot(act, piece, preferred_element_type=jnp.float32)
 
-        pieces_out.append(
-            project(
-                lax.all_gather(specialist_contract_weights[expert], "dp", axis=1, tiled=True),
-                jnp.int32(0),
-            )
-        )
+        pieces_out.append(project(_feed_squares(specialist_contract_weights[expert]), jnp.int32(0)))
     outputs = jnp.stack(pieces_out)
     combined = jnp.zeros((tok_rows, EMBED_DIMENSION), jnp.float32)
     for expert in range(experts):

time: 1090 us -> 950 us (0.87)
  waiting for transfers between devices: 771 us -> 577 us
  starting transfers between devices: 0.55 us -> 33.9 us
  local copies, waits for them, and re-layouts: 55 us -> 68.8 us
    all_gather x4 -> x0, waiting for transfers between devices: 237 us -> none  [body(): lax.all_gather(specialist_contract_weights[expert], 'dp', axis=1, tiled=T...]
    all_to_all x0 -> x4, waiting for transfers between devices: none -> 98.5 us  [_feed_squares(): lax.all_to_all(jnp.stack([work_x for _ in range(lax.psum(1, axis_name='dp...]
    all_gather x1, waiting for transfers between devices: 43.5 us -> 0.02 us  [body(): features = lax.all_gather(normed_local, 'mp', axis=1, tiled=True)]
    all_to_all x0 -> x4, starting transfers between devices: none -> 33.6 us  [_feed_squares(): lax.all_to_all(jnp.stack([work_x for _ in range(lax.psum(1, axis_name='dp...]
    all_gather x4, waiting for transfers between devices: 187 us -> 162 us  [body(): lax.all_gather(specialist_switch_weights[expert], 'dp', axis=0, tiled=True)]
    all_gather x4, waiting for transfers between devices: 227 us -> 243 us  [body(): lax.all_gather(specialist_expand_weights[expert], 'dp', axis=0, tiled=True)]
    unnamed x15 -> x11, waiting for transfers between devices: 76.1 us -> 73.9 us
  transfers between devices with their start and end apart: 14 -> 14, of which waited for: 14 -> 12; matrix products, arithmetic and copies ran while one was open for 9% -> 12% of each run, Pallas kernels for 0% -> 0%
where the time goes in v1:
time: 950 us; the launch traced here: 941 us
  waiting for transfers between devices  577 us (61%)
  blocking collectives  181 us (19%)
  local copies, waits for them, and re-layouts  68.8 us (7%)
  other arithmetic  37.7 us (4%)
  starting transfers between devices  33.9 us (4%)
  matrix products  28 us (3%)
  between operations  15 us (2%)
    all_gather x4, waiting for transfers between devices, body(): lax.all_gather(specialist_expand_weights[expert], 'dp', axis=0, tiled=True)  243 us
    all_gather x4, waiting for transfers between devices, body(): lax.all_gather(specialist_switch_weights[expert], 'dp', axis=0, tiled=True)  162 us
    all_to_all x4, waiting for transfers between devices, _feed_squares(): lax.all_to_all(jnp.stack([work_x for _ in range(lax.psum(1, axis_name='dp...  98.5 us
    unnamed x11, waiting for transfers between devices  73.9 us
    all_gather x2, blocking collectives, body(): held = lax.all_gather(stats, axis, axis=0)  60.6 us
    all_gather x1, blocking collectives, body(): lax.all_gather(end_normed, 'dp', axis=0, tiled=True)  50.6 us
    psum x1, blocking collectives, body(): lax.psum(jnp.sum(skip_stream_arriving * skip_stream_arriving, axis=1), 'mp')  38.4 us
    all_to_all x4, starting transfers between devices, _feed_squares(): lax.all_to_all(jnp.stack([work_x for _ in range(lax.psum(1, axis_name='dp...  33.6 us
  transfers between devices with their start and end apart: 14, of which 12 were waited for; matrix products, arithmetic and copies ran while one was open for 12% of the time, Pallas kernels for 0%

profile of v1, /device:TPU:1, one launch (start us, length us, event | category | flops | bytes accessed | tf_op | source)
XLA Modules:
  0.0 941.2 jit_solution(1800277115857562482)
XLA Ops:
  8.4 38.4 %psum.7 = f32[256]{0:T(256)S(1)} all-reduce(f32[256]{0:T(256)S(1)} %multiply_reduce_fusion), channel_id=1, replica_groups=mesh['dp'=16,'mp'=16] {'mp'}, use_global_device_ids=true, to_apply=%region_5.6 | all-reduce | flops 256 | bytes 2048 | tf_op jit(solution)/shard_map/psum | solution.py:50
  56.2 16.3 %all-to-all-start.1 = ((bf16[16,360,144]{1,2,0:T(8,128)(2,1)}), bf16[16,360,144]{1,2,0:T(8,128)(2,1)}, u32[]{:S(2)}, u32[]{:S(2)}) async-start(bf16[16,360,144]{1,2,0:T(8,128)(2,1)} %stack.31), calls=%async_computation.1 | async-start | bytes 3538944 | tf_op jit(solution)/shard_map/all_to_all | solution.py:14
  73.2 54.7 %all-to-all-done.1 = bf16[16,360,144]{1,2,0:T(8,128)(2,1)} async-done(((bf16[16,360,144]{1,2,0:T(8,128)(2,1)}), bf16[16,360,144]{1,2,0:T(8,128)(2,1)}, u32[]{:S(2)}, u32[]{:S(2)}) %all-to-all-start.1) | async-done | bytes 1658912 | tf_op jit(solution)/shard_map/all_to_all | solution.py:14
  129.3 5.9 all-to-all-start
  137.2 40.5 %all-to-all-done = bf16[16,360,144]{1,2,0:T(8,128)(2,1)} async-done(((bf16[16,360,144]{1,2,0:T(8,128)(2,1)}), bf16[16,360,144]{1,2,0:T(8,128)(2,1)}, u32[]{:S(2)}, u32[]{:S(2)}) %all-to-all-start) | async-done | bytes 1658912 | tf_op jit(solution)/shard_map/all_to_all | solution.py:14
  198.4 10.4 %scatter_custom_fusion.8 = s32[160]{0:T(256)S(1)} fusion(s32[256]{0:T(256)S(1)} %bitcast.168, s32[256]{0:T(256)S(1)} %iota.14, s32[]{:T(128)} %constant.26.clone.1), kind=kCustom, calls=%fused_computation.174 | custom fusion | bytes 644 | tf_op jit(solution)/shard_map/scatter | solution.py:27
  220.7 6.5 all-to-all-start.3
  257.2 16.2 %all-gather.27.cloned.1.call-done = bf16[1,2304,360]{2,1,0:T(8,128)(2,1)} async-done(((bf16[1,144,360]{2,1,0:T(8,128)(2,1)}), bf16[1,2304,360]{2,1,0:T(8,128)(2,1)}) %all-gather.27.cloned.1.call-update) | async-done | bytes 1658896 | tf_op jit(solution)/shard_map/all_gather | solution.py:76
  275.7 70.9 %all-gather.29.cloned.1.call-done = bf16[1,2304,360]{2,1,0:T(8,128)(2,1)} async-done(((bf16[1,144,360]{2,1,0:T(8,128)(2,1)}), bf16[1,2304,360]{2,1,0:T(8,128)(2,1)}) %all-gather.29.cloned.1.call-update) | async-done | bytes 1658896 | tf_op jit(solution)/shard_map/all_gather | solution.py:77
  351.0 5.0 scatter_custom_fusion.3
  356.0 49.4 %all-gather.31.cloned.1.call-done = bf16[1,2304,360]{2,1,0:T(8,128)(2,1)} async-done(((bf16[1,144,360]{2,1,0:T(8,128)(2,1)}), bf16[1,2304,360]{2,1,0:T(8,128)(2,1)}) %all-gather.31.cloned.1.call-update) | async-done | bytes 1658896 | tf_op jit(solution)/shard_map/all_gather | solution.py:76
  407.5 57.4 %all-gather.33.cloned.1.call-done = bf16[1,2304,360]{2,1,0:T(8,128)(2,1)} async-done(((bf16[1,144,360]{2,1,0:T(8,128)(2,1)}), bf16[1,2304,360]{2,1,0:T(8,128)(2,1)}) %all-gather.33.cloned.1.call-update) | async-done | bytes 1658896 | tf_op jit(solution)/shard_map/all_gather | solution.py:77
  469.2 6.5 scatter_fusion
  475.8 47.9 %all-gather.35.cloned.1.call-done = bf16[1,2304,360]{2,1,0:T(8,128)(2,1)} async-done(((bf16[1,144,360]{2,1,0:T(8,128)(2,1)}), bf16[1,2304,360]{2,1,0:T(8,128)(2,1)}) %all-gather.35.cloned.1.call-update) | async-done | bytes 1658896 | tf_op jit(solution)/shard_map/all_gather | solution.py:76
  525.7 57.0 %all-gather.37.cloned.1.call-done = bf16[1,2304,360]{2,1,0:T(8,128)(2,1)} async-done(((bf16[1,144,360]{2,1,0:T(8,128)(2,1)}), bf16[1,2304,360]{2,1,0:T(8,128)(2,1)}) %all-gather.37.cloned.1.call-update) | async-done | bytes 1658896 | tf_op jit(solution)/shard_map/all_gather | solution.py:77
  587.1 6.5 scatter_fusion.1
  593.7 48.0 %all-gather.39.cloned.1.call-done = bf16[1,2304,360]{2,1,0:T(8,128)(2,1)} async-done(((bf16[1,144,360]{2,1,0:T(8,128)(2,1)}), bf16[1,2304,360]{2,1,0:T(8,128)(2,1)}) %all-gather.39.cloned.1.call-update) | async-done | bytes 1658896 | tf_op jit(solution)/shard_map/all_gather | solution.py:76
  643.7 57.5 %all-gather.41.cloned.1.call-done = bf16[1,2304,360]{2,1,0:T(8,128)(2,1)} async-done(((bf16[1,144,360]{2,1,0:T(8,128)(2,1)}), bf16[1,2304,360]{2,1,0:T(8,128)(2,1)}) %all-gather.41.cloned.1.call-update) | async-done | bytes 1658896 | tf_op jit(solution)/shard_map/all_gather | solution.py:77
  705.5 6.5 scatter_fusion.2
  716.6 70.1 %reduce-scatter.4.cloned.1.call-done = bf16[144,256]{1,0:T(8,128)(2,1)} async-done(((bf16[2304,256]{1,0:T(8,128)(2,1)}), bf16[144,256]{1,0:T(8,128)(2,1)}) %reduce-scatter.4.cloned.1.call-update) | async-done | bytes 73744
  789.0 31.6 %all-gather.11 = f32[16,144,4]{1,2,0:T(4,128)S(1)} all-gather(f32[1,144,4]{1,2,0:T(4,128)S(1)} %bitcast.144), channel_id=10, replica_groups=mesh['dp'=16,'mp'=16] {'mp'}, dimensions={0}, use_global_device_ids=true | all-gather | bytes 39168 | tf_op jit(solution)/shard_map/all_gather | solution.py:97
  821.0 50.6 %all-gather.12 = bf16[16,4,2304]{2,1,0:T(4,128)(2,1)S(1)} all-gather(bf16[1,4,2304]{2,1,0:T(4,128)(2,1)S(1)} %fusion.74), channel_id=1, replica_groups=mesh['dp'=16,'mp'=16] {'dp'}, dimensions={0}, use_global_device_ids=true | all-gather | bytes 313344 | tf_op jit(solution)/shard_map/all_gather | solution.py:104
  872.5 29.8 %all-gather.13 = f32[16,2,64]{2,1,0:T(2,128)S(1)} all-gather(f32[1,2,64]{2,1,0:T(2,128)S(1)} %maximum_bitcast_fusion), channel_id=11, replica_groups=mesh['dp'=16,'mp'=16] {'mp'}, dimensions={0}, use_global_device_ids=true | all-gather | bytes 8704 | tf_op jit(solution)/shard_map/all_gather | solution.py:112
  902.4 30.7 %all-gather.14 = f32[16,2,64]{2,1,0:T(2,128)S(1)} all-gather(f32[1,2,64]{2,1,0:T(2,128)S(1)} %maximum_bitcast_fusion.1), channel_id=12, replica_groups=mesh['dp'=16,'mp'=16] {'dp'}, dimensions={0}, use_global_device_ids=true | all-gather | bytes 8704 | tf_op jit(solution)/shard_map/all_gather | solution.py:112
  (180 shorter events, 111.7 us)
Async XLA Ops:
  7.2 864.5 %copy-start = (bf16[2304,512]{1,0:T(8,128)(2,1)S(1)}, bf16[2304,512]{1,0:T(8,128)(2,1)}, u32[]{:S(2)}) copy-start(bf16[2304,512]{1,0:T(8,128)(2,1)} %param.20) | copy-start | bytes 7077892
  7.2 47.6 %copy-start.5 = (bf16[4,360,144]{1,2,0:T(8,128)(2,1)S(1)}, bf16[4,360,144]{1,2,0:T(8,128)(2,1)}, u32[]{:S(2)}) copy-start(bf16[4,360,144]{1,2,0:T(8,128)(2,1)} %param.18) | copy-start | bytes 1244164
  7.2 220.0 %all-gather.25.cloned.1.call-start = ((), (), s32[]{:S(2)}) async-start(), calls=%async_computation.5 | async-start | bytes 1253376 | tf_op jit(solution)/shard_map/all_gather | solution.py:56
  48.5 225.0 %all-gather.27.cloned.1.call-start = ((), (), s32[]{:S(2)}) async-start(), calls=%async_computation.6 | async-start | bytes 1880064 | tf_op jit(solution)/shard_map/all_gather | solution.py:76
  50.4 296.2 %all-gather.29.cloned.1.call-start = ((), (), s32[]{:S(2)}) async-start(), calls=%async_computation.7 | async-start | bytes 1880064 | tf_op jit(solution)/shard_map/all_gather | solution.py:77
  52.3 353.2 %all-gather.31.cloned.1.call-start = ((), (), s32[]{:S(2)}) async-start(), calls=%async_computation.8 | async-start | bytes 1880064 | tf_op jit(solution)/shard_map/all_gather | solution.py:76
  52.9 412.0 %all-gather.33.cloned.1.call-start = ((), (), s32[]{:S(2)}) async-start(), calls=%async_computation.9 | async-start | bytes 1880064 | tf_op jit(solution)/shard_map/all_gather | solution.py:77
  53.4 470.2 %all-gather.35.cloned.1.call-start = ((), (), s32[]{:S(2)}) async-start(), calls=%async_computation.10 | async-start | bytes 1880064 | tf_op jit(solution)/shard_map/all_gather | solution.py:76
  54.0 528.6 %all-gather.37.cloned.1.call-start = ((), (), s32[]{:S(2)}) async-start(), calls=%async_computation.11 | async-start | bytes 1880064 | tf_op jit(solution)/shard_map/all_gather | solution.py:77
  56.2 71.7 %all-to-all-start.1 = ((bf16[16,360,144]{1,2,0:T(8,128)(2,1)}), bf16[16,360,144]{1,2,0:T(8,128)(2,1)}, u32[]{:S(2)}, u32[]{:S(2)}) async-start(bf16[16,360,144]{1,2,0:T(8,128)(2,1)} %stack.31), calls=%async_computation.1 | async-start | bytes 3538944 | tf_op jit(solution)/shard_map/all_to_all | solution.py:14
  72.5 569.1 %all-gather.39.cloned.1.call-start = ((), (), s32[]{:S(2)}) async-start(), calls=%async_computation.12 | async-start | bytes 1880064 | tf_op jit(solution)/shard_map/all_gather | solution.py:76
  129.3 6.7 copy-start.6
  129.3 48.5 %all-to-all-start = ((bf16[16,360,144]{1,2,0:T(8,128)(2,1)}), bf16[16,360,144]{1,2,0:T(8,128)(2,1)}, u32[]{:S(2)}, u32[]{:S(2)}) async-start(bf16[16,360,144]{1,2,0:T(8,128)(2,1)} %stack.30), calls=%async_computation | async-start | bytes 3538944 | tf_op jit(solution)/shard_map/all_to_all | solution.py:14
  135.2 566.0 %all-gather.41.cloned.1.call-start = ((), (), s32[]{:S(2)}) async-start(), calls=%async_computation.13 | async-start | bytes 1880064 | tf_op jit(solution)/shard_map/all_gather | solution.py:77
  179.1 40.2 %all-to-all-start.2 = ((bf16[16,360,144]{1,2,0:T(8,128)(2,1)}), bf16[16,360,144]{1,2,0:T(8,128)(2,1)}, u32[]{:S(2)}, u32[]{:S(2)}) async-start(bf16[16,360,144]{1,2,0:T(8,128)(2,1)} %stack.32), calls=%async_computation.2 | async-start | bytes 3538944 | tf_op jit(solution)/shard_map/all_to_all | solution.py:14
  214.2 6.4 copy-start.15
  220.7 6.6 copy-start.7
  220.7 423.0 %all-to-all-start.3 = ((bf16[16,360,144]{1,2,0:T(8,128)(2,1)}), bf16[16,360,144]{1,2,0:T(8,128)(2,1)}, u32[]{:S(2)}, u32[]{:S(2)}) async-start(bf16[16,360,144]{1,2,0:T(8,128)(2,1)} %stack.33), calls=%async_computation.3 | async-start | bytes 3538944 | tf_op jit(solution)/shard_map/all_to_all | solution.py:14
  227.2 559.5 %reduce-scatter.4.cloned.1.call-start = ((), (), s32[]{:S(2)}) async-start(), calls=%async_computation.14 | async-start | bytes 1253376
  254.4 92.2 %copy-start.4 = (bf16[160,2304]{1,0:T(8,128)(2,1)S(1)}, bf16[160,2304]{1,0:T(8,128)(2,1)}, u32[]{:S(2)}) copy-start(bf16[160,2304]{1,0:T(8,128)(2,1)} %gather_fusion) | copy-start | bytes 2211844
  351.0 54.5 %copy-start.3 = (bf16[160,2304]{1,0:T(8,128)(2,1)S(1)}, bf16[160,2304]{1,0:T(8,128)(2,1)}, u32[]{:S(2)}) copy-start(bf16[160,2304]{1,0:T(8,128)(2,1)} %gather_fusion.2) | copy-start | bytes 2211844
  469.2 54.5 %copy-start.2 = (bf16[160,2304]{1,0:T(8,128)(2,1)S(1)}, bf16[160,2304]{1,0:T(8,128)(2,1)}, u32[]{:S(2)}) copy-start(bf16[160,2304]{1,0:T(8,128)(2,1)} %gather_fusion.4) | copy-start | bytes 2211844
  587.1 54.5 %copy-start.1 = (bf16[160,2304]{1,0:T(8,128)(2,1)S(1)}, bf16[160,2304]{1,0:T(8,128)(2,1)}, u32[]{:S(2)}) copy-start(bf16[160,2304]{1,0:T(8,128)(2,1)} %gather_fusion.6) | copy-start | bytes 2211844
  715.3 105.7 %copy-start.8 = (f32[2304]{0:T(1024)S(1)}, f32[2304]{0:T(1024)}, u32[]{:S(2)}) copy-start(f32[2304]{0:T(1024)} %param.19) | copy-start | bytes 27652
  (8 other events, 25.8 us)
Sparse Core Ops, SparseCore 0:
  48.6 119.7 all-gather.24
  171.0 102.4 all-gather.26
  276.1 70.4 all-gather.28
  349.1 56.3 all-gather.30
  408.5 56.3 all-gather.32
  467.3 56.3 all-gather.34
  526.3 56.3 all-gather.36
  585.3 56.3 all-gather.38
  644.8 56.3 all-gather.40
  715.4 71.2 reduce-scatter.3
